TPU v7x, 32 devices: a whole 2x2x4 slice. The times are simulated.
32 devices in a mesh: dp: 2 (over x), seq: 16 (over z, y, core).
Axes of the slice: x: 2, y: 2, z: 4, core: 2. Of those that a mesh axis runs over, the one named last changes fastest.
Arguments:
- hidden_in: bfloat16 [2, 3072, 3584], P('dp', 'seq'), may hold values from -6 to 6
- spike_level: int32 [2, 3072], P('dp', 'seq'), may hold values from 1 to 4
- value_weight: bfloat16 [3584, 256], P('dp'), may hold values from -0.09375 to 0.09375
- queries: bfloat16 [2, 3072, 1792], P('dp', 'seq'), may hold values from -32 to 32
- key_states: bfloat16 [2, 3072, 256], P('dp', 'seq'), may hold values from -32 to 32
- spike_mask: int32 [2, 3072, 14], P('dp', 'seq'), may hold values 0 or 1
- out_grad: bfloat16 [2, 3072, 1792], P('dp', 'seq'), may hold values from -6 to 6
Outputs:
- query_grad: bfloat16 [2, 3072, 1792], P('dp', 'seq')
- key_grad: bfloat16 [2, 3072, 256], P('dp', 'seq')
- value_weight_grad: bfloat16 [3584, 256], P('dp')
All inputs are finite; a program needn't handle non-finite values. No bound on the sum of `spike_mask` on one device may be relied on, other than what follows from the above.
Results may differ from a plain program's by a relative error of at most 0.012.
The roundings to bfloat16 on the way count: a program that leaves them out, or rounds other values in their place, can miss the bound.
Values may be sent and summed in bfloat16 or wider, within the bound.
No kernel may reach another device: no remote copies, remote signals or barrier semaphores. Data moves between devices by JAX's collectives and lax.ppermute only.
A program may use at most 64 MiB of HBM per device.

v0:
```python
import math
import jax
import jax.numpy as jnp
from jax import lax
from jax.sharding import PartitionSpec as P

QH = 14
KVH = 2
HD = 128
WINDOW = 512
LEVELS = 4
GROUP = 7
masked_score = -1e30


def shifted(value, axis, steps):
    count = lax.axis_size(axis)
    first, last = (max(0, -steps), min(count, count - steps))
    return lax.ppermute(value, axis, [(source, source + steps) for source in range(first, last)])


def body(hidden_in, spike_level, value_weight, queries, key_states, spike_mask, out_grad):
    tok_rows = hidden_in.shape[1]
    reach_blocks = (WINDOW + tok_rows - 2) // tok_rows
    key_span = (reach_blocks + 1) * tok_rows
    score_scale = 1.0 / math.sqrt(HD)
    position = lax.axis_index("seq")
    spiked = (
        hidden_in[0].astype(jnp.float32) * (spike_level[0].astype(jnp.float32) / LEVELS)[:, None]
    ).astype(jnp.bfloat16)
    values = jnp.dot(
        spiked,
        lax.all_gather(value_weight, "dp", axis=0, tiled=True),
        preferred_element_type=jnp.float32,
    ).astype(jnp.bfloat16)
    own_keys = key_states[0]
    key_pieces = []
    value_pieces = []
    for offset in range(reach_blocks, 0, -1):
        got_keys, got_values = shifted((own_keys, values), "seq", offset)
        key_pieces.append(got_keys)
        value_pieces.append(got_values)
    key_block = jnp.concatenate(key_pieces + [own_keys], axis=0)
    value_block = jnp.concatenate(value_pieces + [values], axis=0)
    query_pos = position * tok_rows + jnp.arange(tok_rows, dtype=jnp.int32)
    key_pos = position * tok_rows - reach_blocks * tok_rows + jnp.arange(key_span, dtype=jnp.int32)
    allowed = (
        (key_pos[None, :] <= query_pos[:, None])
        & (key_pos[None, :] > query_pos[:, None] - WINDOW)
        & (key_pos[None, :] >= 0)
    )
    gated = (
        out_grad[0].reshape(tok_rows, QH, HD) * spike_mask[0][:, :, None].astype(jnp.bfloat16)
    ).reshape(tok_rows, KVH, GROUP, HD)
    query_heads = queries[0].reshape(tok_rows, KVH, GROUP, HD)
    query_parts = []
    key_parts = []
    value_parts = []
    for group in range(KVH):
        query_grp = query_heads[:, group]
        gated_grp = gated[:, group]
        key_grp = key_block[:, group * HD : (group + 1) * HD]
        value_grp = value_block[:, group * HD : (group + 1) * HD]
        scores = (
            jnp.einsum("thd,jd->htj", query_grp, key_grp, preferred_element_type=jnp.float32)
            * score_scale
        )
        scores = jnp.where(allowed[None], scores, masked_score)
        highest = jnp.max(scores, axis=-1, keepdims=True)
        expo = jnp.exp(scores - highest)
        probs = expo / jnp.sum(expo, axis=-1, keepdims=True)
        rounded_probs = probs.astype(jnp.bfloat16)
        attended = jnp.einsum(
            "htj,jd->thd", rounded_probs, value_grp, preferred_element_type=jnp.float32
        )
        delta = jnp.sum(gated_grp.astype(jnp.float32) * attended, axis=-1)
        prob_grad = jnp.einsum(
            "thd,jd->htj", gated_grp, value_grp, preferred_element_type=jnp.float32
        )
        score_grad = (probs * (prob_grad - jnp.transpose(delta)[:, :, None])).astype(jnp.bfloat16)
        query_part = (
            jnp.einsum("htj,jd->thd", score_grad, key_grp, preferred_element_type=jnp.float32)
            * score_scale
        )
        query_parts.append(query_part.astype(jnp.bfloat16))
        key_parts.append(
            jnp.einsum("htj,thd->jd", score_grad, query_grp, preferred_element_type=jnp.float32)
            * score_scale
        )
        value_parts.append(
            jnp.einsum("htj,thd->jd", rounded_probs, gated_grp, preferred_element_type=jnp.float32)
        )
    query_grad = jnp.stack(query_parts, axis=1).reshape(tok_rows, QH * HD)
    key_terms = jnp.concatenate(key_parts, axis=1)
    value_terms = jnp.concatenate(value_parts, axis=1)
    key_total = key_terms[reach_blocks * tok_rows :]
    value_total = value_terms[reach_blocks * tok_rows :]
    for offset in range(1, reach_blocks + 1):
        first_row = (reach_blocks - offset) * tok_rows
        back_keys, back_values = shifted(
            (
                key_terms[first_row : first_row + tok_rows],
                value_terms[first_row : first_row + tok_rows],
            ),
            "seq",
            -offset,
        )
        key_total = key_total + back_keys
        value_total = value_total + back_values
    value_grad = value_total.astype(jnp.bfloat16)
    whole_term = lax.dot_general(
        spiked, value_grad, (((0,), (0,)), ((), ())), preferred_element_type=jnp.float32
    )
    summed = lax.psum(whole_term, "seq")
    owned = lax.psum_scatter(summed, "dp", scatter_dimension=0, tiled=True)
    return (query_grad[None], key_total.astype(jnp.bfloat16)[None], owned.astype(jnp.bfloat16))


def solution(mesh):
    placed = (
        P("dp", "seq", None),
        P("dp", "seq"),
        P("dp", None),
        P("dp", "seq", None),
        P("dp", "seq", None),
        P("dp", "seq", None),
        P("dp", "seq", None),
    )
    return jax.shard_map(
        body,
        mesh=mesh,
        in_specs=placed,
        out_specs=(P("dp", "seq", None), P("dp", "seq", None), P("dp", None)),
        check_vma=False,
    )
```

profile of v0, /device:TPU:0, one launch (start us, length us, event | category | flops | bytes accessed | tf_op | source)
XLA Modules:
  0.0 193.0 jit_solution(12145091537902446400)
XLA Ops:
  7.2 2.5 %collective-permute-start.2 = (bf16[192,256]{1,0:T(8,128)(2,1)}, bf16[192,256]{1,0:T(8,128)(2,1)S(1)}, u32[]{:S(2)}, u32[]{:S(2)}) collective-permute-start(bf16[192,256]{1,0:T(8,128)(2,1)} %bitcast.156), channel_id=1, source_target_pairs={{0,1},{1,2},{2,3},{3,4},{4,5},{5,6},{6,7},{7,8},{8,9},{9,10},{10,1... | collective-permute-start | bytes 294920 | tf_op jit(solution)/shard_map/ppermute | solution.py:19
  9.7 4.4 %collective-permute-start.1 = (bf16[192,256]{1,0:T(8,128)(2,1)}, bf16[192,256]{1,0:T(8,128)(2,1)S(1)}, u32[]{:S(2)}, u32[]{:S(2)}) collective-permute-start(bf16[192,256]{1,0:T(8,128)(2,1)} %bitcast.157), channel_id=1, source_target_pairs={{0,2},{1,3},{2,4},{3,5},{4,6},{5,7},{6,8},{7,9},{8,10},{9,11},{10,... | collective-permute-start | bytes 294920 | tf_op jit(solution)/shard_map/ppermute | solution.py:19
  14.2 5.0 %collective-permute-start = (bf16[192,256]{1,0:T(8,128)(2,1)}, bf16[192,256]{1,0:T(8,128)(2,1)}, u32[]{:S(2)}, u32[]{:S(2)}) collective-permute-start(bf16[192,256]{1,0:T(8,128)(2,1)} %bitcast.158), channel_id=1, source_target_pairs={{0,3},{1,4},{2,5},{3,6},{4,7},{5,8},{6,9},{7,10},{8,11},{9,12},{10... | collective-permute-start | bytes 294920 | tf_op jit(solution)/shard_map/ppermute | solution.py:19
  19.3 0.8 convert_reduce_fusion
  20.1 1.9 reshape_squeeze.6
  22.1 0.8 reshape_squeeze.7
  22.9 0.4 copy_multiply_fusion
  23.5 0.6 copy-done.10
  24.2 0.6 copy-done.11
  24.8 1.1 pad_maximum_fusion.1
  26.0 3.5 %fusion.59 = (f32[7,192]{1,0:T(8,128)S(1)}, f32[7,192,768]{2,1,0:T(8,128)}) fusion(pred[192,768]{1,0:T(8,128)(4,1)S(1)} %and_and_fusion, bf16[192,1,7,128]{3,2,1,0:T(8,128)(2,1)S(1)} %get-tuple-element.15, bf16[768,256]{1,0:T(8,128)(2,1)S(1)} %pad_maximum_fusion.1), kind=kOutput, calls=%fused_computation.105 | convolution fusion | flops 268370688 | bytes 4871424 | tf_op jit(solution)/shard_map/sub | solution.py:70
  29.5 2.5 %fusion.15 = bf16[7,192,768]{2,1,0:T(8,128)(2,1)S(1)} fusion(f32[7,192,768]{2,1,0:T(8,128)} %get-tuple-element.20, f32[7,192]{1,0:T(8,128)S(1)} %get-tuple-element.19), kind=kLoop, calls=%fused_computation.24 | loop fusion | flops 2064384 | bytes 6198528 | tf_op jit(solution)/shard_map/convert_element_type | solution.py:72
  32.0 4.4 %fusion.58 = (f32[7,192]{1,0:T(8,128)S(1)}, f32[7,192,768]{2,1,0:T(8,128)}) fusion(pred[192,768]{1,0:T(8,128)(4,1)} %copy-done.9, bf16[192,1,7,128]{3,2,1,0:T(8,128)(2,1)S(1)} %get-tuple-element.16, bf16[768,256]{1,0:T(8,128)(2,1)S(1)} %pad_maximum_fusion.1), kind=kOutput, calls=%fused_computation.104 | convolution fusion | flops 268370688 | bytes 4871424 | tf_op jit(solution)/shard_map/sub | solution.py:70
  36.5 0.5 convolution_bitcast_fusion.3
  37.0 1.6 copy-done
  39.0 0.5 convolution_bitcast_fusion.2
  39.6 0.7 copy-done.3
  40.3 1.3 collective-permute-start.9
  41.6 1.3 collective-permute-start.11
  42.9 1.3 collective-permute-start.10
  44.3 8.4 %collective-permute-done.11 = f32[192,256]{0,1:T(8,128)S(1)} collective-permute-done((f32[192,256]{0,1:T(8,128)S(1)}, f32[192,256]{0,1:T(8,128)S(1)}, u32[]{:S(2)}, u32[]{:S(2)}) %collective-permute-start.11) | collective-permute-done | bytes 196640 | tf_op jit(solution)/shard_map/ppermute | solution.py:19
  52.7 2.0 %collective-permute-done.10 = f32[192,256]{0,1:T(8,128)S(1)} collective-permute-done((f32[192,256]{0,1:T(8,128)S(1)}, f32[192,256]{0,1:T(8,128)S(1)}, u32[]{:S(2)}, u32[]{:S(2)}) %collective-permute-start.10) | collective-permute-done | bytes 196640 | tf_op jit(solution)/shard_map/ppermute | solution.py:19
  54.7 2.7 %fusion.27 = f32[3584,256]{1,0:T(8,128)} fusion(bf16[1,192,3584]{2,1,0:T(8,128)(2,1)S(1)} %copy-done.5, f32[192]{0:T(256)S(1)} %bitcast.160, f32[192,256]{0,1:T(8,128)S(1)} %collective-permute-done.11, f32[192,256]{0,1:T(8,128)S(1)} %collective-permute-done.10, f32[192,256]{0,1:T(8,128)S(1)} %collective-permute-done.9, ...), kind=kOutput, calls=%fused_computation.60 | convolution fusion | flops 354631680 | bytes 6423296 | tf_op jit(solution)/shard_map/dot_general | solution.py:111
  57.4 2.6 %convolution_convert_fusion = bf16[192,256]{1,0:T(8,128)(2,1)S(1)} fusion(bf16[3584,256]{1,0:T(8,128)(2,1)} %all-gather.2.cloned.1.call-done, bf16[1,192,3584]{2,1,0:T(8,128)(2,1)} %param.7, f32[192]{0:T(256)} %bitcast.161), kind=kOutput, calls=%fused_computation.44 | convolution fusion | flops 354435072 | bytes 3310336 | tf_op jit(solution)/shard_map/dot_general | solution.py:31
  60.1 3.5 %collective-permute-start.5 = (bf16[192,256]{1,0:T(8,128)(2,1)S(1)}, bf16[192,256]{1,0:T(8,128)(2,1)S(1)}, u32[]{:S(2)}, u32[]{:S(2)}) collective-permute-start(bf16[192,256]{1,0:T(8,128)(2,1)S(1)} %convolution_convert_fusion), channel_id=1, source_target_pairs={{0,1},{1,2},{2,3},{3,4},{4,5},{5,6},{6,7},{7,8},{8,9},{9,10},{10,1... | collective-permute-start | bytes 294920 | tf_op jit(solution)/shard_map/ppermute | solution.py:19
  63.6 5.9 %collective-permute-start.4 = (bf16[192,256]{1,0:T(8,128)(2,1)S(1)}, bf16[192,256]{1,0:T(8,128)(2,1)S(1)}, u32[]{:S(2)}, u32[]{:S(2)}) collective-permute-start(bf16[192,256]{1,0:T(8,128)(2,1)S(1)} %convolution_convert_fusion), channel_id=1, source_target_pairs={{0,2},{1,3},{2,4},{3,5},{4,6},{5,7},{6,8},{7,9},{8,10},{9,11},{10,... | collective-permute-start | bytes 294920 | tf_op jit(solution)/shard_map/ppermute | solution.py:19
  69.6 4.7 %collective-permute-start.3 = (bf16[192,256]{1,0:T(8,128)(2,1)S(1)}, bf16[192,256]{1,0:T(8,128)(2,1)S(1)}, u32[]{:S(2)}, u32[]{:S(2)}) collective-permute-start(bf16[192,256]{1,0:T(8,128)(2,1)S(1)} %convolution_convert_fusion), channel_id=1, source_target_pairs={{0,3},{1,4},{2,5},{3,6},{4,7},{5,8},{6,9},{7,10},{8,11},{9,12},{10... | collective-permute-start | bytes 294920 | tf_op jit(solution)/shard_map/ppermute | solution.py:19
  74.3 2.0 %collective-permute-done.3 = bf16[192,256]{1,0:T(8,128)(2,1)S(1)} collective-permute-done((bf16[192,256]{1,0:T(8,128)(2,1)S(1)}, bf16[192,256]{1,0:T(8,128)(2,1)S(1)}, u32[]{:S(2)}, u32[]{:S(2)}) %collective-permute-start.3) | collective-permute-done | bytes 98336 | tf_op jit(solution)/shard_map/ppermute | solution.py:19
  76.3 0.8 fusion.23
  77.1 0.8 fusion.24
  77.9 0.5 copy-done.2
  78.4 1.0 fusion.5
  79.5 0.5 fusion.22
  80.1 1.7 copy-done.1
  81.8 1.0 fusion.3
  82.8 0.5 fusion.21
  83.5 1.3 collective-permute-start.6
  84.8 1.3 collective-permute-start.8
  86.1 1.3 collective-permute-start.7
  87.4 0.7 fusion.26
  88.1 0.7 fusion.25
  88.9 0.5 copy.14
  89.3 1.6 broadcast_in_dim_reshape.3
  90.9 4.6 %collective-permute-done.8 = f32[192,256]{0,1:T(8,128)S(1)} collective-permute-done((f32[192,256]{0,1:T(8,128)S(1)}, f32[192,256]{0,1:T(8,128)S(1)}, u32[]{:S(2)}, u32[]{:S(2)}) %collective-permute-start.8) | collective-permute-done | bytes 196640 | tf_op jit(solution)/shard_map/ppermute | solution.py:19
  95.6 1.6 collective-permute-done.7
  97.3 0.7 copy.15
  98.0 12.7 %reduce-scatter.2.cloned.1.call-done = f32[1792,256]{1,0:T(8,128)} async-done(((f32[3584,256]{1,0:T(8,128)}), f32[1792,256]{1,0:T(8,128)}) %reduce-scatter.2.cloned.1.call-update) | async-done | bytes 1835024 | tf_op jit(solution)/shard_map/reduce_scatter | solution.py:115
  110.8 75.4 %all-reduce.1 = bf16[1792,256]{1,0:T(8,128)(2,1)} all-reduce(f32[1792,256]{1,0:T(8,128)} %reduce-scatter.2.cloned.1.call-done), channel_id=1, replica_groups=mesh['dp'=2,'seq'=16] {'seq'}, use_global_device_ids=true, to_apply=%region_6.7 | all-reduce | flops 458752 | bytes 2752512 | tf_op jit(solution)/shard_map/psum | solution.py:114
  (47 shorter events, 1.3 us)
Async XLA Ops:
  7.2 14.9 %copy-start.6 = (bf16[1,192,1792]{2,1,0:T(8,128)(2,1)S(1)}, bf16[1,192,1792]{2,1,0:T(8,128)(2,1)}, u32[]{:S(2)}) copy-start(bf16[1,192,1792]{2,1,0:T(8,128)(2,1)} %param.13) | copy-start | bytes 2064388
  7.2 50.3 %all-gather.2.cloned.1.call-start = ((), (), s32[]{:S(2)}) async-start(), calls=%async_computation.1 | async-start | bytes 2752512 | tf_op jit(solution)/shard_map/all_gather | solution.py:33
  7.2 16.3 %collective-permute-start.2 = (bf16[192,256]{1,0:T(8,128)(2,1)}, bf16[192,256]{1,0:T(8,128)(2,1)S(1)}, u32[]{:S(2)}, u32[]{:S(2)}) collective-permute-start(bf16[192,256]{1,0:T(8,128)(2,1)} %bitcast.156), channel_id=1, source_target_pairs={{0,1},{1,2},{2,3},{3,4},{4,5},{5,6},{6,7},{7,8},{8,9},{9,10},{10,1... | collective-permute-start | bytes 294920 | tf_op jit(solution)/shard_map/ppermute | solution.py:19
  9.7 13.8 %collective-permute-start.1 = (bf16[192,256]{1,0:T(8,128)(2,1)}, bf16[192,256]{1,0:T(8,128)(2,1)S(1)}, u32[]{:S(2)}, u32[]{:S(2)}) collective-permute-start(bf16[192,256]{1,0:T(8,128)(2,1)} %bitcast.157), channel_id=1, source_target_pairs={{0,2},{1,3},{2,4},{3,5},{4,6},{5,7},{6,8},{7,9},{8,10},{9,11},{10,... | collective-permute-start | bytes 294920 | tf_op jit(solution)/shard_map/ppermute | solution.py:19
  14.2 10.7 %collective-permute-start = (bf16[192,256]{1,0:T(8,128)(2,1)}, bf16[192,256]{1,0:T(8,128)(2,1)}, u32[]{:S(2)}, u32[]{:S(2)}) collective-permute-start(bf16[192,256]{1,0:T(8,128)(2,1)} %bitcast.158), channel_id=1, source_target_pairs={{0,3},{1,4},{2,5},{3,6},{4,7},{5,8},{6,9},{7,10},{8,11},{9,12},{10... | collective-permute-start | bytes 294920 | tf_op jit(solution)/shard_map/ppermute | solution.py:19
  19.2 91.6 %reduce-scatter.2.cloned.1.call-start = ((), (), s32[]{:S(2)}) async-start(), calls=%async_computation.2 | async-start | bytes 5505024 | tf_op jit(solution)/shard_map/reduce_scatter | solution.py:115
  22.1 7.5 %copy-start.7 = (bf16[192,1,7,128]{3,2,1,0:T(8,128)(2,1)}, bf16[192,1,7,128]{3,2,1,0:T(8,128)(2,1)S(1)}, u32[]{:S(2)}) copy-start(bf16[192,1,7,128]{3,2,1,0:T(8,128)(2,1)S(1)} %get-tuple-element.15) | copy-start | bytes 1032196
  23.5 6.0 %copy-start.9 = (pred[192,768]{1,0:T(8,128)(4,1)}, pred[192,768]{1,0:T(8,128)(4,1)S(1)}, u32[]{:S(2)}) copy-start(pred[192,768]{1,0:T(8,128)(4,1)S(1)} %and_and_fusion) | copy-start | bytes 442372
  23.5 0.7 copy-start.10
  24.2 0.6 copy-start.11
  36.4 2.2 %copy-start = (f32[7,192,768]{2,1,0:T(8,128)S(1)}, f32[7,192,768]{2,1,0:T(8,128)}, u32[]{:S(2)}) copy-start(f32[7,192,768]{2,1,0:T(8,128)} %get-tuple-element.18) | copy-start | bytes 12386308
  38.9 1.4 copy-start.3
  39.0 5.3 %copy-start.13 = (s32[1,192]{1,0:T(1,128)S(1)}, s32[1,192]{1,0:T(1,128)}, u32[]{:S(2)}) copy-start(s32[1,192]{1,0:T(1,128)} %param.8) | copy-start | bytes 2308
  39.0 15.8 %copy-start.5 = (bf16[1,192,3584]{2,1,0:T(8,128)(2,1)S(1)}, bf16[1,192,3584]{2,1,0:T(8,128)(2,1)}, u32[]{:S(2)}) copy-start(bf16[1,192,3584]{2,1,0:T(8,128)(2,1)} %param.7) | copy-start | bytes 4128772
  40.3 3.9 %collective-permute-start.9 = (f32[192,256]{0,1:T(8,128)S(1)}, f32[192,256]{0,1:T(8,128)S(1)}, u32[]{:S(2)}, u32[]{:S(2)}) collective-permute-start(f32[192,256]{0,1:T(8,128)S(1)} %get-tuple-element.9), channel_id=1, source_target_pairs={{1,0},{2,1},{3,2},{4,3},{5,4},{6,5},{7,6},{8,7},{9,8},{10,9},{11,1... | collective-permute-start | bytes 589832 | tf_op jit(solution)/shard_map/ppermute | solution.py:19
  41.6 11.1 %collective-permute-start.11 = (f32[192,256]{0,1:T(8,128)S(1)}, f32[192,256]{0,1:T(8,128)S(1)}, u32[]{:S(2)}, u32[]{:S(2)}) collective-permute-start(f32[192,256]{0,1:T(8,128)S(1)} %get-tuple-element.10), channel_id=1, source_target_pairs={{3,0},{4,1},{5,2},{6,3},{7,4},{8,5},{9,6},{10,7},{11,8},{12,9},{13... | collective-permute-start | bytes 589832 | tf_op jit(solution)/shard_map/ppermute | solution.py:19
  42.9 11.8 %collective-permute-start.10 = (f32[192,256]{0,1:T(8,128)S(1)}, f32[192,256]{0,1:T(8,128)S(1)}, u32[]{:S(2)}, u32[]{:S(2)}) collective-permute-start(f32[192,256]{0,1:T(8,128)S(1)} %get-tuple-element.11), channel_id=1, source_target_pairs={{2,0},{3,1},{4,2},{5,3},{6,4},{7,5},{8,6},{9,7},{10,8},{11,9},{12,... | collective-permute-start | bytes 589832 | tf_op jit(solution)/shard_map/ppermute | solution.py:19
  44.2 10.5 %copy-start.12 = (f32[1,192]{1,0:T(1,128)}, f32[1,192]{1,0:T(1,128)S(1)}, u32[]{:S(2)}) copy-start(f32[1,192]{1,0:T(1,128)S(1)} %convert_multiply_fusion.1) | copy-start | bytes 2308
  57.4 19.7 %copy-start.4 = (bf16[7,192,768]{2,1,0:T(8,128)(2,1)S(1)}, bf16[7,192,768]{2,1,0:T(8,128)(2,1)}, u32[]{:S(2)}) copy-start(bf16[7,192,768]{2,1,0:T(8,128)(2,1)} %copy-done.3) | copy-start | bytes 6193156
  60.1 14.1 %collective-permute-start.5 = (bf16[192,256]{1,0:T(8,128)(2,1)S(1)}, bf16[192,256]{1,0:T(8,128)(2,1)S(1)}, u32[]{:S(2)}, u32[]{:S(2)}) collective-permute-start(bf16[192,256]{1,0:T(8,128)(2,1)S(1)} %convolution_convert_fusion), channel_id=1, source_target_pairs={{0,1},{1,2},{2,3},{3,4},{4,5},{5,6},{6,7},{7,8},{8,9},{9,10},{10,1... | collective-permute-start | bytes 294920 | tf_op jit(solution)/shard_map/ppermute | solution.py:19
  63.6 10.6 %collective-permute-start.4 = (bf16[192,256]{1,0:T(8,128)(2,1)S(1)}, bf16[192,256]{1,0:T(8,128)(2,1)S(1)}, u32[]{:S(2)}, u32[]{:S(2)}) collective-permute-start(bf16[192,256]{1,0:T(8,128)(2,1)S(1)} %convolution_convert_fusion), channel_id=1, source_target_pairs={{0,2},{1,3},{2,4},{3,5},{4,6},{5,7},{6,8},{7,9},{8,10},{9,11},{10,... | collective-permute-start | bytes 294920 | tf_op jit(solution)/shard_map/ppermute | solution.py:19
  69.6 6.7 %collective-permute-start.3 = (bf16[192,256]{1,0:T(8,128)(2,1)S(1)}, bf16[192,256]{1,0:T(8,128)(2,1)S(1)}, u32[]{:S(2)}, u32[]{:S(2)}) collective-permute-start(bf16[192,256]{1,0:T(8,128)(2,1)S(1)} %convolution_convert_fusion), channel_id=1, source_target_pairs={{0,3},{1,4},{2,5},{3,6},{4,7},{5,8},{6,9},{7,10},{8,11},{9,12},{10... | collective-permute-start | bytes 294920 | tf_op jit(solution)/shard_map/ppermute | solution.py:19
  76.3 2.2 %copy-start.2 = (f32[7,192,768]{2,1,0:T(8,128)S(1)}, f32[7,192,768]{2,1,0:T(8,128)}, u32[]{:S(2)}) copy-start(f32[7,192,768]{2,1,0:T(8,128)} %get-tuple-element.20) | copy-start | bytes 12386308
  78.4 1.1 copy-start.8
  79.5 2.3 %copy-start.1 = (f32[7,192,768]{2,1,0:T(8,128)S(1)}, f32[7,192,768]{2,1,0:T(8,128)}, u32[]{:S(2)}) copy-start(f32[7,192,768]{2,1,0:T(8,128)} %get-tuple-element.18) | copy-start | bytes 12386308
  83.5 7.4 %collective-permute-start.6 = (f32[192,256]{0,1:T(8,128)S(1)}, f32[192,256]{0,1:T(8,128)S(1)}, u32[]{:S(2)}, u32[]{:S(2)}) collective-permute-start(f32[192,256]{0,1:T(8,128)S(1)} %get-tuple-element.12), channel_id=1, source_target_pairs={{1,0},{2,1},{3,2},{4,3},{5,4},{6,5},{7,6},{8,7},{9,8},{10,9},{11,1... | collective-permute-start | bytes 589832 | tf_op jit(solution)/shard_map/ppermute | solution.py:19
  84.8 10.8 %collective-permute-start.8 = (f32[192,256]{0,1:T(8,128)S(1)}, f32[192,256]{0,1:T(8,128)S(1)}, u32[]{:S(2)}, u32[]{:S(2)}) collective-permute-start(f32[192,256]{0,1:T(8,128)S(1)} %get-tuple-element.13), channel_id=1, source_target_pairs={{3,0},{4,1},{5,2},{6,3},{7,4},{8,5},{9,6},{10,7},{11,8},{12,9},{13... | collective-permute-start | bytes 589832 | tf_op jit(solution)/shard_map/ppermute | solution.py:19
  86.1 11.0 %collective-permute-start.7 = (f32[192,256]{0,1:T(8,128)S(1)}, f32[192,256]{0,1:T(8,128)S(1)}, u32[]{:S(2)}, u32[]{:S(2)}) collective-permute-start(f32[192,256]{0,1:T(8,128)S(1)} %get-tuple-element.14), channel_id=1, source_target_pairs={{2,0},{3,1},{4,2},{5,3},{6,4},{7,5},{8,6},{9,7},{10,8},{11,9},{12,... | collective-permute-start | bytes 589832 | tf_op jit(solution)/shard_map/ppermute | solution.py:19
Sparse Core Ops, SparseCore 0:
  19.3 28.8 all-gather.1
  57.5 53.1 reduce-scatter.1
where the time goes:
time: 194 us; the launch traced here: 193 us
  blocking collectives  75.4 us (39%)
  starting transfers between devices  33.9 us (17%)
  waiting for transfers between devices  31.4 us (16%)
  matrix products  20.5 us (11%)
  between operations  14.5 us (7%)
  local copies, waits for them, and re-layouts  11.5 us (6%)
  other arithmetic  5.85 us (3%)
    psum x1, blocking collectives, body(): summed = lax.psum(whole_term, 'seq')  75.4 us
    ppermute x12, starting transfers between devices, shifted(): lax.ppermute(value, axis, [(source, source + steps) for source in range(f...  33.8 us
    ppermute x12, waiting for transfers between devices, shifted(): lax.ppermute(value, axis, [(source, source + steps) for source in range(f...  18.7 us
    reduce_scatter x1, waiting for transfers between devices, body(): owned = lax.psum_scatter(summed, 'dp', scatter_dimension=0, tiled=True)  12.7 us
    sub x2, matrix products, body(): expo = jnp.exp(scores - highest)  7.97 us
    unnamed x29, local copies, waits for them, and re-layouts  6.66 us
  transfers between devices with their start and end apart: 14, of which 6 were waited for; matrix products, arithmetic and copies ran while one was open for 17% of the time, Pallas kernels for 0%

commit v1 on v0

--- a/solution.py
+++ b/solution.py
@@ -111,7 +111,9 @@
     whole_term = lax.dot_general(
         spiked, value_grad, (((0,), (0,)), ((), ())), preferred_element_type=jnp.float32
     )
-    summed = lax.psum(whole_term, "seq")
+    summed = whole_term
+    for hop in (1, 2, 4, 8):
+        summed = summed + lax.ppermute(summed, "seq", [(dev, dev ^ hop) for dev in range(16)])
     owned = lax.psum_scatter(summed, "dp", scatter_dimension=0, tiled=True)
     return (query_grad[None], key_total.astype(jnp.bfloat16)[None], owned.astype(jnp.bfloat16))
 

time: 194 us -> 455 us (2.35)
  waiting for transfers between devices: 31.4 us -> 356 us
  blocking collectives: 75.4 us -> 0 us
  other arithmetic: 5.85 us -> 17 us
    ppermute x0 -> x4, waiting for transfers between devices: none -> 322 us  [body(): lax.ppermute(summed, 'seq', [(dev, dev ^ hop) for dev in range(16)])]
    psum x1 -> x0, blocking collectives: 75.4 us -> none  [body(): summed = lax.psum(whole_term, 'seq')]
    ppermute x0 -> x4, starting transfers between devices: none -> 10.3 us  [body(): lax.ppermute(summed, 'seq', [(dev, dev ^ hop) for dev in range(16)])]
    add x0 -> x4, other arithmetic: none -> 8.67 us  [body(): summed + lax.ppermute(summed, 'seq', [(dev, dev ^ hop) for dev in range(1...]
    ppermute x12, starting transfers between devices: 33.8 us -> 27.2 us  [shifted(): lax.ppermute(value, axis, [(source, source + steps) for source in range(f...]
  transfers between devices with their start and end apart: 14 -> 18, of which waited for: 6 -> 10; matrix products, arithmetic and copies ran while one was open for 17% -> 5% of each run, Pallas kernels for 0% -> 0%
where the time goes in v1:
time: 455 us; the launch traced here: 454 us
  waiting for transfers between devices  356 us (78%)
  starting transfers between devices  37.5 us (8%)
  matrix products  17.8 us (4%)
  other arithmetic  17 us (4%)
  between operations  14.5 us (3%)
  local copies, waits for them, and re-layouts  11.2 us (2%)
    ppermute x4, waiting for transfers between devices, body(): lax.ppermute(summed, 'seq', [(dev, dev ^ hop) for dev in range(16)])  322 us
    ppermute x12, starting transfers between devices, shifted(): lax.ppermute(value, axis, [(source, source + steps) for source in range(f...  27.2 us
    ppermute x12, waiting for transfers between devices, shifted(): lax.ppermute(value, axis, [(source, source + steps) for source in range(f...  18.6 us
    reduce_scatter x1, waiting for transfers between devices, body(): owned = lax.psum_scatter(summed, 'dp', scatter_dimension=0, tiled=True)  15 us
    ppermute x4, starting transfers between devices, body(): lax.ppermute(summed, 'seq', [(dev, dev ^ hop) for dev in range(16)])  10.3 us
  transfers between devices with their start and end apart: 18, of which 10 were waited for; matrix products, arithmetic and copies ran while one was open for 5% of the time, Pallas kernels for 0%

profile of v1, /device:TPU:0, one launch (start us, length us, event | category | flops | bytes accessed | tf_op | source)
XLA Modules:
  0.0 453.8 jit_solution(10303124283824031351)
XLA Ops:
  7.2 2.5 collective-permute-start.2
  9.7 4.4 collective-permute-start.1
  14.2 5.0 %collective-permute-start = (bf16[192,256]{1,0:T(8,128)(2,1)}, bf16[192,256]{1,0:T(8,128)(2,1)}, u32[]{:S(2)}, u32[]{:S(2)}) collective-permute-start(bf16[192,256]{1,0:T(8,128)(2,1)} %bitcast.158), channel_id=1, source_target_pairs={{0,3},{1,4},{2,5},{3,6},{4,7},{5,8},{6,9},{7,10},{8,11},{9,12},{10... | collective-permute-start | bytes 294920 | tf_op jit(solution)/shard_map/ppermute | solution.py:19
  19.2 0.8 convert_reduce_fusion
  20.0 1.9 reshape_squeeze.6
  22.0 0.8 reshape_squeeze.7
  24.7 1.1 pad_maximum_fusion.1
  25.8 3.5 fusion.59
  29.3 3.5 fusion.58
  32.9 2.5 fusion.15
  35.9 1.6 copy-done
  39.1 1.3 collective-permute-start.9
  40.4 1.3 collective-permute-start.11
  41.7 1.3 collective-permute-start.10
  43.1 8.4 %collective-permute-done.11 = f32[192,256]{0,1:T(8,128)S(1)} collective-permute-done((f32[192,256]{0,1:T(8,128)S(1)}, f32[192,256]{0,1:T(8,128)S(1)}, u32[]{:S(2)}, u32[]{:S(2)}) %collective-permute-start.11) | collective-permute-done | bytes 196640 | tf_op jit(solution)/shard_map/ppermute | solution.py:19
  51.5 2.0 collective-permute-done.10
  53.5 0.8 fusion.27
  54.4 1.7 collective-permute-start.12
  56.0 6.0 %collective-permute-done.12 = f32[3584,256]{1,0:T(8,128)S(1)} collective-permute-done((f32[3584,256]{1,0:T(8,128)S(1)}, f32[3584,256]{1,0:T(8,128)S(1)}, u32[]{:S(2)}, u32[]{:S(2)}) %collective-permute-start.12) | collective-permute-done | bytes 3670048 | tf_op jit(solution)/shard_map/ppermute | solution.py:116
  62.6 4.3 collective-permute-start.13
  66.9 79.6 %collective-permute-done.13 = f32[3584,256]{1,0:T(8,128)S(1)} collective-permute-done((f32[3584,256]{1,0:T(8,128)S(1)}, f32[3584,256]{1,0:T(8,128)S(1)}, u32[]{:S(2)}, u32[]{:S(2)}) %collective-permute-start.13) | collective-permute-done | bytes 3670048 | tf_op jit(solution)/shard_map/ppermute | solution.py:116
  147.0 1.8 collective-permute-start.14
  148.9 79.1 %collective-permute-done.14 = f32[3584,256]{1,0:T(8,128)S(1)} collective-permute-done((f32[3584,256]{1,0:T(8,128)S(1)}, f32[3584,256]{1,0:T(8,128)S(1)}, u32[]{:S(2)}, u32[]{:S(2)}) %collective-permute-start.14) | collective-permute-done | bytes 3670048 | tf_op jit(solution)/shard_map/ppermute | solution.py:116
  228.0 2.3 add.77
  230.3 2.4 collective-permute-start.15
  232.8 157.4 %collective-permute-done.15 = f32[3584,256]{1,0:T(8,128)} collective-permute-done((f32[3584,256]{1,0:T(8,128)}, f32[3584,256]{1,0:T(8,128)}, u32[]{:S(2)}, u32[]{:S(2)}) %collective-permute-start.15) | collective-permute-done | bytes 3670048 | tf_op jit(solution)/shard_map/ppermute | solution.py:116
  390.1 5.4 %add.78 = f32[3584,256]{1,0:T(8,128)} add(f32[3584,256]{1,0:T(8,128)} %add.77, f32[3584,256]{1,0:T(8,128)} %collective-permute-done.15) | non-fusion elementwise | flops 917504 | bytes 11010048 | tf_op jit(solution)/shard_map/add | solution.py:116
  395.6 2.6 convolution_convert_fusion
  398.3 1.3 collective-permute-start.5
  399.6 3.6 collective-permute-start.4
  403.2 2.6 collective-permute-start.3
  405.8 2.0 collective-permute-done.3
  407.8 0.8 fusion.23
  408.7 0.8 fusion.24
  410.0 1.0 fusion.5
  411.6 1.6 copy-done.1
  413.2 1.0 fusion.3
  415.0 1.3 collective-permute-start.6
  416.3 1.3 collective-permute-start.8
  417.6 1.3 collective-permute-start.7
  418.9 0.7 fusion.26
  419.6 0.7 fusion.25
  420.8 1.6 broadcast_in_dim_reshape.3
  422.4 4.8 %collective-permute-done.8 = f32[192,256]{0,1:T(8,128)S(1)} collective-permute-done((f32[192,256]{0,1:T(8,128)S(1)}, f32[192,256]{0,1:T(8,128)S(1)}, u32[]{:S(2)}, u32[]{:S(2)}) %collective-permute-start.8) | collective-permute-done | bytes 196640 | tf_op jit(solution)/shard_map/ppermute | solution.py:19
  427.2 1.4 collective-permute-done.7
  428.7 0.7 copy.15
  429.5 15.0 %reduce-scatter.2.cloned.1.call-done = f32[1792,256]{1,0:T(8,128)} async-done(((f32[3584,256]{1,0:T(8,128)}), f32[1792,256]{1,0:T(8,128)}) %reduce-scatter.2.cloned.1.call-update) | async-done | bytes 1835024 | tf_op jit(solution)/shard_map/reduce_scatter | solution.py:117
  444.5 2.5 convert_element_type.89
  (57 shorter events, 7.6 us)
Async XLA Ops:
  7.2 14.8 %copy-start.6 = (bf16[1,192,1792]{2,1,0:T(8,128)(2,1)S(1)}, bf16[1,192,1792]{2,1,0:T(8,128)(2,1)}, u32[]{:S(2)}) copy-start(bf16[1,192,1792]{2,1,0:T(8,128)(2,1)} %param.13) | copy-start | bytes 2064388
  7.2 388.5 %all-gather.2.cloned.1.call-start = ((), (), s32[]{:S(2)}) async-start(), calls=%async_computation.1 | async-start | bytes 2752512 | tf_op jit(solution)/shard_map/all_gather | solution.py:33
  7.2 16.2 %collective-permute-start.2 = (bf16[192,256]{1,0:T(8,128)(2,1)}, bf16[192,256]{1,0:T(8,128)(2,1)S(1)}, u32[]{:S(2)}, u32[]{:S(2)}) collective-permute-start(bf16[192,256]{1,0:T(8,128)(2,1)} %bitcast.156), channel_id=1, source_target_pairs={{0,1},{1,2},{2,3},{3,4},{4,5},{5,6},{6,7},{7,8},{8,9},{9,10},{10,1... | collective-permute-start | bytes 294920 | tf_op jit(solution)/shard_map/ppermute | solution.py:19
  9.7 13.7 %collective-permute-start.1 = (bf16[192,256]{1,0:T(8,128)(2,1)}, bf16[192,256]{1,0:T(8,128)(2,1)S(1)}, u32[]{:S(2)}, u32[]{:S(2)}) collective-permute-start(bf16[192,256]{1,0:T(8,128)(2,1)} %bitcast.157), channel_id=1, source_target_pairs={{0,2},{1,3},{2,4},{3,5},{4,6},{5,7},{6,8},{7,9},{8,10},{9,11},{10,... | collective-permute-start | bytes 294920 | tf_op jit(solution)/shard_map/ppermute | solution.py:19
  14.2 10.5 %collective-permute-start = (bf16[192,256]{1,0:T(8,128)(2,1)}, bf16[192,256]{1,0:T(8,128)(2,1)}, u32[]{:S(2)}, u32[]{:S(2)}) collective-permute-start(bf16[192,256]{1,0:T(8,128)(2,1)} %bitcast.158), channel_id=1, source_target_pairs={{0,3},{1,4},{2,5},{3,6},{4,7},{5,8},{6,9},{7,10},{8,11},{9,12},{10... | collective-permute-start | bytes 294920 | tf_op jit(solution)/shard_map/ppermute | solution.py:19
  22.0 7.3 %copy-start.7 = (bf16[192,1,7,128]{3,2,1,0:T(8,128)(2,1)}, bf16[192,1,7,128]{3,2,1,0:T(8,128)(2,1)S(1)}, u32[]{:S(2)}) copy-start(bf16[192,1,7,128]{3,2,1,0:T(8,128)(2,1)S(1)} %get-tuple-element.15) | copy-start | bytes 1032196
  23.4 0.6 copy-start.9
  24.1 0.6 copy-start.10
  35.4 2.2 copy-start
  37.8 1.3 copy-start.3
  37.9 5.2 %copy-start.12 = (s32[1,192]{1,0:T(1,128)S(1)}, s32[1,192]{1,0:T(1,128)}, u32[]{:S(2)}) copy-start(s32[1,192]{1,0:T(1,128)} %param.8) | copy-start | bytes 2308
  37.9 15.6 %copy-start.5 = (bf16[1,192,3584]{2,1,0:T(8,128)(2,1)S(1)}, bf16[1,192,3584]{2,1,0:T(8,128)(2,1)}, u32[]{:S(2)}) copy-start(bf16[1,192,3584]{2,1,0:T(8,128)(2,1)} %param.7) | copy-start | bytes 4128772
  39.1 3.9 collective-permute-start.9
  40.4 11.1 %collective-permute-start.11 = (f32[192,256]{0,1:T(8,128)S(1)}, f32[192,256]{0,1:T(8,128)S(1)}, u32[]{:S(2)}, u32[]{:S(2)}) collective-permute-start(f32[192,256]{0,1:T(8,128)S(1)} %get-tuple-element.10), channel_id=1, source_target_pairs={{3,0},{4,1},{5,2},{6,3},{7,4},{8,5},{9,6},{10,7},{11,8},{12,9},{13... | collective-permute-start | bytes 589832 | tf_op jit(solution)/shard_map/ppermute | solution.py:19
  41.7 11.8 %collective-permute-start.10 = (f32[192,256]{0,1:T(8,128)S(1)}, f32[192,256]{0,1:T(8,128)S(1)}, u32[]{:S(2)}, u32[]{:S(2)}) collective-permute-start(f32[192,256]{0,1:T(8,128)S(1)} %get-tuple-element.11), channel_id=1, source_target_pairs={{2,0},{3,1},{4,2},{5,3},{6,4},{7,5},{8,6},{9,7},{10,8},{11,9},{12,... | collective-permute-start | bytes 589832 | tf_op jit(solution)/shard_map/ppermute | solution.py:19
  43.0 11.3 %copy-start.11 = (f32[1,192]{1,0:T(1,128)}, f32[1,192]{1,0:T(1,128)S(1)}, u32[]{:S(2)}) copy-start(f32[1,192]{1,0:T(1,128)S(1)} %convert_multiply_fusion.1) | copy-start | bytes 2308
  54.4 7.7 %collective-permute-start.12 = (f32[3584,256]{1,0:T(8,128)S(1)}, f32[3584,256]{1,0:T(8,128)S(1)}, u32[]{:S(2)}, u32[]{:S(2)}) collective-permute-start(f32[3584,256]{1,0:T(8,128)S(1)} %fusion.27), channel_id=1, source_target_pairs={{0,1},{1,0},{2,3},{3,2},{4,5},{5,4},{6,7},{7,6},{8,9},{9,8},{10,11... | collective-permute-start | bytes 11010056 | tf_op jit(solution)/shard_map/ppermute | solution.py:116
  62.6 84.0 %collective-permute-start.13 = (f32[3584,256]{1,0:T(8,128)S(1)}, f32[3584,256]{1,0:T(8,128)S(1)}, u32[]{:S(2)}, u32[]{:S(2)}) collective-permute-start(f32[3584,256]{1,0:T(8,128)S(1)} %add.75), channel_id=1, source_target_pairs={{0,2},{1,3},{2,0},{3,1},{4,6},{5,7},{6,4},{7,5},{8,10},{9,11},{10,... | collective-permute-start | bytes 11010056 | tf_op jit(solution)/shard_map/ppermute | solution.py:116
  147.0 81.0 %collective-permute-start.14 = (f32[3584,256]{1,0:T(8,128)S(1)}, f32[3584,256]{1,0:T(8,128)S(1)}, u32[]{:S(2)}, u32[]{:S(2)}) collective-permute-start(f32[3584,256]{1,0:T(8,128)S(1)} %add.76), channel_id=1, source_target_pairs={{0,4},{1,5},{2,6},{3,7},{4,0},{5,1},{6,2},{7,3},{8,12},{9,13},{10,... | collective-permute-start | bytes 11010056 | tf_op jit(solution)/shard_map/ppermute | solution.py:116
  230.3 159.9 %collective-permute-start.15 = (f32[3584,256]{1,0:T(8,128)}, f32[3584,256]{1,0:T(8,128)}, u32[]{:S(2)}, u32[]{:S(2)}) collective-permute-start(f32[3584,256]{1,0:T(8,128)} %add.77), channel_id=1, source_target_pairs={{0,8},{1,9},{2,10},{3,11},{4,12},{5,13},{6,14},{7,15},{8,0},{9,1},... | collective-permute-start | bytes 11010056 | tf_op jit(solution)/shard_map/ppermute | solution.py:116
  232.7 211.8 %reduce-scatter.2.cloned.1.call-start = ((), (), s32[]{:S(2)}) async-start(), calls=%async_computation.2 | async-start | bytes 5505024 | tf_op jit(solution)/shard_map/reduce_scatter | solution.py:117
  395.6 13.0 %copy-start.4 = (bf16[7,192,768]{2,1,0:T(8,128)(2,1)S(1)}, bf16[7,192,768]{2,1,0:T(8,128)(2,1)}, u32[]{:S(2)}) copy-start(bf16[7,192,768]{2,1,0:T(8,128)(2,1)} %copy-done.3) | copy-start | bytes 6193156
  398.3 7.5 %collective-permute-start.5 = (bf16[192,256]{1,0:T(8,128)(2,1)S(1)}, bf16[192,256]{1,0:T(8,128)(2,1)S(1)}, u32[]{:S(2)}, u32[]{:S(2)}) collective-permute-start(bf16[192,256]{1,0:T(8,128)(2,1)S(1)} %convolution_convert_fusion), channel_id=1, source_target_pairs={{0,1},{1,2},{2,3},{3,4},{4,5},{5,6},{6,7},{7,8},{8,9},{9,10},{10,1... | collective-permute-start | bytes 294920 | tf_op jit(solution)/shard_map/ppermute | solution.py:19
  399.6 6.2 %collective-permute-start.4 = (bf16[192,256]{1,0:T(8,128)(2,1)S(1)}, bf16[192,256]{1,0:T(8,128)(2,1)S(1)}, u32[]{:S(2)}, u32[]{:S(2)}) collective-permute-start(bf16[192,256]{1,0:T(8,128)(2,1)S(1)} %convolution_convert_fusion), channel_id=1, source_target_pairs={{0,2},{1,3},{2,4},{3,5},{4,6},{5,7},{6,8},{7,9},{8,10},{9,11},{10,... | collective-permute-start | bytes 294920 | tf_op jit(solution)/shard_map/ppermute | solution.py:19
  403.2 4.6 %collective-permute-start.3 = (bf16[192,256]{1,0:T(8,128)(2,1)S(1)}, bf16[192,256]{1,0:T(8,128)(2,1)S(1)}, u32[]{:S(2)}, u32[]{:S(2)}) collective-permute-start(bf16[192,256]{1,0:T(8,128)(2,1)S(1)} %convolution_convert_fusion), channel_id=1, source_target_pairs={{0,3},{1,4},{2,5},{3,6},{4,7},{5,8},{6,9},{7,10},{8,11},{9,12},{10... | collective-permute-start | bytes 294920 | tf_op jit(solution)/shard_map/ppermute | solution.py:19
  407.8 2.2 copy-start.2
  410.0 1.1 copy-start.8
  411.1 2.2 copy-start.1
  415.0 7.5 %collective-permute-start.6 = (f32[192,256]{0,1:T(8,128)S(1)}, f32[192,256]{0,1:T(8,128)S(1)}, u32[]{:S(2)}, u32[]{:S(2)}) collective-permute-start(f32[192,256]{0,1:T(8,128)S(1)} %get-tuple-element.12), channel_id=1, source_target_pairs={{1,0},{2,1},{3,2},{4,3},{5,4},{6,5},{7,6},{8,7},{9,8},{10,9},{11,1... | collective-permute-start | bytes 589832 | tf_op jit(solution)/shard_map/ppermute | solution.py:19
  416.3 10.9 %collective-permute-start.8 = (f32[192,256]{0,1:T(8,128)S(1)}, f32[192,256]{0,1:T(8,128)S(1)}, u32[]{:S(2)}, u32[]{:S(2)}) collective-permute-start(f32[192,256]{0,1:T(8,128)S(1)} %get-tuple-element.13), channel_id=1, source_target_pairs={{3,0},{4,1},{5,2},{6,3},{7,4},{8,5},{9,6},{10,7},{11,8},{12,9},{13... | collective-permute-start | bytes 589832 | tf_op jit(solution)/shard_map/ppermute | solution.py:19
  417.6 11.0 %collective-permute-start.7 = (f32[192,256]{0,1:T(8,128)S(1)}, f32[192,256]{0,1:T(8,128)S(1)}, u32[]{:S(2)}, u32[]{:S(2)}) collective-permute-start(f32[192,256]{0,1:T(8,128)S(1)} %get-tuple-element.14), channel_id=1, source_target_pairs={{2,0},{3,1},{4,2},{5,3},{6,4},{7,5},{8,6},{9,7},{10,8},{11,9},{12,... | collective-permute-start | bytes 589832 | tf_op jit(solution)/shard_map/ppermute | solution.py:19
Sparse Core Ops, SparseCore 0:
  232.8 29.3 all-gather.1
  395.7 48.7 reduce-scatter.1
